TPU v7x, 32 devices: a whole 2x2x4 slice. The times are simulated.
32 devices in a mesh: space: 8 (over z, y), view: 4 (over x, core).
Axes of the slice: x: 2, y: 2, z: 4, core: 2. Of those that a mesh axis runs over, the one named last changes fastest.
Arguments:
- params: float32 [59, 16384], P(None, 'space'), may hold values from -8 to 514, as said below
- visible: int32 [8, 128, 16], P('space'), may hold values from 0 to 2047, as said below
- blocks: int32 [8, 128], P('space'), may hold values from 0 to 63, as said below
- counts: int32 [8, 8], P('space'), may hold values from 1 to 16
- depth_rank: int32 [4, 8], P('view'), may hold values from 0 to 7, each once within a row
- camera: float32 [4, 3], P('view'), may hold values from -0.006 to 0.006
- background: float32 [4, 3], P('view'), may hold values from 0 to 1
- target: float32 [4, 3, 128, 512], P('view', None, 'space'), may hold values from 0 to 1
Outputs:
- grad_params: float32 [59, 16384], P(None, 'space')
- rendered: float32 [4, 3, 128, 512], P('view', None, 'space')
- loss: float32 [4], P('view')
Inputs may be any that keep to these rules, and one draw needn't show every extreme that they name: `visible`: each row of a subspace's table lists 16 different splats of that subspace in increasing order; every splat of the subspace is listed exactly once. Slot j of a subspace goes to owner j // 16; the 16 slots that one subspace sends to one owner name different blocks. counts[s, o] live slots lead the 16 slots that subspace s sends to owner o. `params`: rows 6 to 9 of a column hold a quaternion whose first component lies in [1, 2].
All inputs are finite; a program needn't handle non-finite values.
Results may differ from a plain program's by a relative error of at most 0.0003.
Values sent between devices are 32-bit elements; how exact they have to be, the bound alone decides.
A program may use at most 64 MiB of HBM per device.

v0:
```python
import math
import jax
import jax.numpy as jnp
from jax import lax
from jax.sharding import PartitionSpec as P

HIGHEST = lax.Precision.HIGHEST
SH_ZERO = 0.28209479177387814
SH_ONE = 0.4886025119029199
SH_TWO = (
    1.0925484305920792,
    -1.0925484305920792,
    0.31539156525252005,
    -1.0925484305920792,
    0.5462742152960396,
)
SH_THREE = (
    -0.5900435899266435,
    2.890611442640554,
    -0.4570457994644658,
    0.3731763325901154,
    -0.4570457994644658,
    1.445305721320277,
    -0.5900435899266435,
)
DILATION = 0.3
SMOOTHING = 0.0001
SSIM_FIRST = 0.0001
SSIM_SECOND = 0.0009


def with_halo(x, sides, width):
    for axis, dim in sides:
        devices, length = (lax.axis_size(axis), x.shape[dim])
        up = [(i, (i + 1) % devices) for i in range(devices - 1)]
        down = [(j, i) for i, j in up]
        last = lax.slice_in_dim(x, length - width, length, axis=dim)
        first = lax.slice_in_dim(x, 0, width, axis=dim)
        before = lax.ppermute(last, axis, up)
        after = lax.ppermute(first, axis, down)
        x = jnp.concatenate([before, x, after], axis=dim)
    return x


def passed_along(x, axis, by):
    devices = lax.axis_size(axis)
    pairs = [(i, i + by) for i in range(devices) if 0 <= i + by < devices]
    return lax.ppermute(x, axis, pairs)


def camera_rotation(angles):
    cos_a, sin_a = (jnp.cos(angles[0]), jnp.sin(angles[0]))
    cos_b, sin_b = (jnp.cos(angles[1]), jnp.sin(angles[1]))
    cos_c, sin_c = (jnp.cos(angles[2]), jnp.sin(angles[2]))
    unity = jnp.ones_like(cos_a)
    nought = jnp.zeros_like(cos_a)
    turn_x = jnp.stack(
        [
            jnp.stack([unity, nought, nought]),
            jnp.stack([nought, cos_a, -sin_a]),
            jnp.stack([nought, sin_a, cos_a]),
        ]
    )
    turn_y = jnp.stack(
        [
            jnp.stack([cos_b, nought, sin_b]),
            jnp.stack([nought, unity, nought]),
            jnp.stack([-sin_b, nought, cos_b]),
        ]
    )
    turn_z = jnp.stack(
        [
            jnp.stack([cos_c, -sin_c, nought]),
            jnp.stack([sin_c, cos_c, nought]),
            jnp.stack([nought, nought, unity]),
        ]
    )
    return jnp.dot(jnp.dot(turn_z, turn_y, precision=HIGHEST), turn_x, precision=HIGHEST)


def harmonics(view_axis):
    axis_x, axis_y, axis_z = (view_axis[0], view_axis[1], view_axis[2])
    sq_x, sq_y, sq_z = (axis_x * axis_x, axis_y * axis_y, axis_z * axis_z)
    values = [
        SH_ZERO * jnp.ones_like(axis_x),
        -SH_ONE * axis_y,
        SH_ONE * axis_z,
        -SH_ONE * axis_x,
        SH_TWO[0] * axis_x * axis_y,
        SH_TWO[1] * axis_y * axis_z,
        SH_TWO[2] * (2.0 * sq_z - sq_x - sq_y),
        SH_TWO[3] * axis_x * axis_z,
        SH_TWO[4] * (sq_x - sq_y),
        SH_THREE[0] * axis_y * (3.0 * sq_x - sq_y),
        SH_THREE[1] * axis_x * axis_y * axis_z,
        SH_THREE[2] * axis_y * (4.0 * sq_z - sq_x - sq_y),
        SH_THREE[3] * axis_z * (2.0 * sq_z - 3.0 * sq_x - 3.0 * sq_y),
        SH_THREE[4] * axis_x * (4.0 * sq_z - sq_x - sq_y),
        SH_THREE[5] * axis_z * (sq_x - sq_y),
        SH_THREE[6] * axis_x * (sq_x - 3.0 * sq_y),
    ]
    return jnp.stack(values)


def project(param_in, angles, centre_x, centre_y):
    turn = camera_rotation(angles)
    scales = jnp.exp(param_in[3:6])
    quaternion = param_in[6:10]
    quaternion = quaternion / jnp.sqrt(jnp.sum(quaternion * quaternion, axis=0))
    part_w, part_x, part_y, part_z = (quaternion[0], quaternion[1], quaternion[2], quaternion[3])
    spin = [
        [
            1.0 - 2.0 * (part_y * part_y + part_z * part_z),
            2.0 * (part_x * part_y - part_w * part_z),
            2.0 * (part_x * part_z + part_w * part_y),
        ],
        [
            2.0 * (part_x * part_y + part_w * part_z),
            1.0 - 2.0 * (part_x * part_x + part_z * part_z),
            2.0 * (part_y * part_z - part_w * part_x),
        ],
        [
            2.0 * (part_x * part_z - part_w * part_y),
            2.0 * (part_y * part_z + part_w * part_x),
            1.0 - 2.0 * (part_x * part_x + part_y * part_y),
        ],
    ]
    frame = [
        [
            (
                turn[row, 0] * spin[0][col]
                + turn[row, 1] * spin[1][col]
                + turn[row, 2] * spin[2][col]
            )
            * scales[col]
            for col in range(3)
        ]
        for row in range(2)
    ]
    cov_xx = (
        frame[0][0] * frame[0][0] + frame[0][1] * frame[0][1] + frame[0][2] * frame[0][2] + DILATION
    )
    cov_xy = frame[0][0] * frame[1][0] + frame[0][1] * frame[1][1] + frame[0][2] * frame[1][2]
    cov_yy = (
        frame[1][0] * frame[1][0] + frame[1][1] * frame[1][1] + frame[1][2] * frame[1][2] + DILATION
    )
    determinant = cov_xx * cov_yy - cov_xy * cov_xy
    shift_x = param_in[0] - centre_x
    shift_y = param_in[1] - centre_y
    mean_u = turn[0, 0] * shift_x + turn[0, 1] * shift_y + turn[0, 2] * param_in[2] + centre_x
    mean_w = turn[1, 0] * shift_x + turn[1, 1] * shift_y + turn[1, 2] * param_in[2] + centre_y
    opacity = jax.nn.sigmoid(param_in[10])
    basis = harmonics(turn[2])
    coeffs = param_in[11:59].reshape(16, 3, param_in.shape[1])
    colour = 0.5 + jnp.sum(basis[:, None, None] * coeffs, axis=0)
    record = jnp.stack(
        [mean_u, mean_w, cov_yy / determinant, -cov_xy / determinant, cov_xx / determinant, opacity]
    )
    return jnp.concatenate([record, colour], axis=0)


def make_projector(view_angles, centre_x, centre_y):

    def apply(param_in):
        return project(param_in, view_angles, centre_x, centre_y)

    return apply


def render(gathered, grid_x, grid_y):
    delta_x = grid_x[:, None, :] - gathered[0][:, :, None]
    delta_y = grid_y[:, None, :] - gathered[1][:, :, None]
    powers = 0.5 * (
        gathered[2][:, :, None] * delta_x * delta_x
        + 2.0 * gathered[3][:, :, None] * delta_x * delta_y
        + gathered[4][:, :, None] * delta_y * delta_y
    )
    alphas = gathered[5][:, :, None] * jnp.exp(-powers)
    kept_log = jnp.log1p(-alphas)
    before = jnp.cumsum(kept_log, axis=1) - kept_log
    weights = alphas * jnp.exp(before)
    colour = jnp.einsum("skp,csk->scp", weights, gathered[6:9], precision=HIGHEST)
    return jnp.concatenate([colour, jnp.sum(kept_log, axis=1)[:, None, :]], axis=1)


def pixel_grid(owners, blocks_used, strip_rows, block_cols):
    inner = jnp.arange(128, dtype=jnp.int32)
    corner_y = owners * strip_rows + blocks_used // block_cols * 8
    corner_x = blocks_used % block_cols * 16
    grid_y = (corner_y[:, None] + inner[None, :] // 16).astype(jnp.float32) + 0.5
    grid_x = (corner_x[:, None] + inner[None, :] % 16).astype(jnp.float32) + 0.5
    return (grid_x, grid_y)


def composite(pieces, target_ids, depth_ranks, backdrop, block_rows, block_cols):
    block_count = block_rows * block_cols
    onehot = (
        target_ids[:, :, None] == jnp.arange(block_count, dtype=jnp.int32)[None, None, :]
    ).astype(jnp.float32)
    dense = jnp.einsum("scb,scqp->bsqp", onehot, pieces, precision=HIGHEST)
    kept_log = dense[:, :, 3]
    nearer = (depth_ranks[None, :] < depth_ranks[:, None]).astype(jnp.float32)
    before = jnp.einsum("st,btp->bsp", nearer, kept_log, precision=HIGHEST)
    picture = jnp.einsum("bsp,bscp->bcp", jnp.exp(before), dense[:, :, 0:3], precision=HIGHEST)
    picture = picture + backdrop[None, :, None] * jnp.exp(jnp.sum(kept_log, axis=1))[:, None, :]
    picture = picture.reshape(block_rows, block_cols, 3, 8, 16).transpose(2, 0, 3, 1, 4)
    return picture.reshape(3, block_rows * 8, block_cols * 16)


def blur_taps():
    raw_taps = [math.exp(-(offset - 5) * (offset - 5) / 4.5) for offset in range(11)]
    total = sum(raw_taps)
    return [value / total for value in raw_taps]


def blur(values, count):
    taps = blur_taps()
    width_px = values.shape[2]
    padded = jnp.pad(values, ((0, 0), (0, 0), (5, 5)))
    across = taps[0] * padded[:, :, 0:width_px]
    for offset in range(1, 11):
        across = across + taps[offset] * padded[:, :, offset : offset + width_px]
    result = taps[0] * across[:, 0:count]
    for offset in range(1, 11):
        result = result + taps[offset] * across[:, offset : offset + count]
    return result


def pixel_terms(picture, goal, count):
    mean_a = blur(picture, count)
    mean_b = blur(goal, count)
    var_a = blur(picture * picture, count) - mean_a * mean_a
    var_b = blur(goal * goal, count) - mean_b * mean_b
    cov_ab = blur(picture * goal, count) - mean_a * mean_b
    ssim = (
        (2.0 * mean_a * mean_b + SSIM_FIRST)
        * (2.0 * cov_ab + SSIM_SECOND)
        / ((mean_a * mean_a + mean_b * mean_b + SSIM_FIRST) * (var_a + var_b + SSIM_SECOND))
    )
    differ = picture[:, 5 : 5 + count] - goal[:, 5 : 5 + count]
    return 0.8 * jnp.sqrt(differ * differ + SMOOTHING) + 0.2 * (1.0 - ssim)


def shards(params, visible, blocks, counts, depth_rank, camera, background, target):
    devices = lax.axis_size("space")
    me_index = lax.axis_index("space")
    slot_total = visible.shape[1]
    list_length = visible.shape[2]
    capacity = slot_total // devices
    strip_rows = target.shape[2]
    width_px = target.shape[3]
    block_rows = strip_rows // 8
    block_cols = width_px // 16
    height_px = strip_rows * devices
    lists = visible[0]
    slot_blocks = blocks[0]
    live = jnp.arange(capacity, dtype=jnp.int32)[None, :] < counts[0][:, None]
    target_ids = jnp.where(live, slot_blocks.reshape(devices, capacity), -1)
    centre_x = 0.5 * width_px
    centre_y = 0.5 * height_px
    records, pull_project = jax.vjp(make_projector(camera[0], centre_x, centre_y), params)

    def sender_side(record_in):
        picked = record_in[:, lists]
        return picked.reshape(9, devices, capacity * list_length).transpose(1, 0, 2)

    message, pull_sender = jax.vjp(sender_side, records)
    received, recv_ids = (
        lax.all_to_all(message, "space", split_axis=0, concat_axis=0, tiled=True),
        lax.all_to_all(target_ids, "space", split_axis=0, concat_axis=0, tiled=True),
    )
    own_blocks = jnp.maximum(recv_ids.reshape(devices * capacity), 0)
    grid_x, grid_y = pixel_grid(
        jnp.full(own_blocks.shape, me_index, jnp.int32), own_blocks, strip_rows, block_cols
    )

    def owner_side(recv_in):
        gathered = (
            recv_in.reshape(devices, 9, capacity, list_length)
            .transpose(1, 0, 2, 3)
            .reshape(9, devices * capacity, list_length)
        )
        pieces = render(gathered, grid_x, grid_y).reshape(devices, capacity, 4, 128)
        return composite(pieces, recv_ids, depth_rank[0], background[0], block_rows, block_cols)

    strip, pull_owner = jax.vjp(owner_side, received)
    stacked = jnp.concatenate([strip, target[0]], axis=0)
    extended = with_halo(stacked, (("space", 1),), 5)
    goal = extended[3:6]

    def local_sum(picture):
        return jnp.sum(pixel_terms(picture, goal, strip_rows))

    own_loss, pull_terms = jax.vjp(local_sum, extended[0:3])
    grad_extended = pull_terms(jnp.ones((), jnp.float32))[0]
    from_below = passed_along(grad_extended[:, 0:5], "space", -1)
    from_above = passed_along(grad_extended[:, strip_rows + 5 : strip_rows + 10], "space", 1)
    grad_strip = grad_extended[:, 5 : strip_rows + 5]
    grad_strip = grad_strip.at[:, strip_rows - 5 :].add(from_below).at[:, 0:5].add(from_above)
    grad_received = pull_owner(grad_strip)[0]
    returned = lax.all_to_all(grad_received, "space", split_axis=0, concat_axis=0, tiled=True)
    grad_records = pull_sender(returned)[0]
    grad_params = lax.psum(pull_project(grad_records)[0], "view")
    loss_sum = lax.psum(own_loss, "space")
    loss_value = (loss_sum / (3.0 * height_px * width_px)).reshape(1)
    return (grad_params, strip[None], loss_value)


def solution(mesh):
    in_specs = (
        P(None, "space"),
        P("space", None, None),
        P("space", None),
        P("space", None),
        P("view", None),
        P("view", None),
        P("view", None),
        P("view", None, "space", None),
    )
    out_specs = (P(None, "space"), P("view", None, "space", None), P("view"))
    return jax.shard_map(shards, mesh=mesh, in_specs=in_specs, out_specs=out_specs, check_vma=False)
```

profile of v0, /device:TPU:0, one launch (start us, length us, event | category | flops | bytes accessed | tf_op | source)
XLA Modules:
  0.0 244.3 jit_solution(11177102204411708343)
XLA Ops:
  9.9 7.3 %all-to-all-start = ((s32[8,1,16]{2,1,0:T(1,128)}), s32[8,1,16]{2,1,0:T(1,128)S(1)}, u32[]{:S(2)}, u32[]{:S(2)}) async-start(s32[8,1,16]{2,1,0:T(1,128)} %bitcast.45), calls=%async_computation | async-start | bytes 8192 | tf_op jit(solution)/shard_map/all_to_all | solution.py:270
  38.9 4.8 %add_divide_fusion = (f32[1,2048]{1,0:T(1,128)S(1)}, f32[1,2048]{1,0:T(1,128)S(1)}, f32[1,2048]{1,0:T(1,128)S(1)}) fusion(f32[59,2048]{1,0:T(8,128)} %param.12, f32[]{:T(128)} %bitcast.50, f32[]{:T(128)} %bitcast.49, f32[]{:T(128)} %bitcast.48, f32[]{:T(128)} %bitcast.53, f32[]{:T(128)} %bitcast.52, f32[]{:T(128)} %bitcast.51), kind=kLoop, calls=%fused_computation.484 | loop fusion | flops 34816 | bytes 57368 | tf_op jit(solution)/shard_map/jvp()/div | solution.py:152
  55.5 4.6 %fusion.269 = (f32[1,2048]{1,0:T(1,128)S(1)}, f32[1,2048]{1,0:T(1,128)S(1)}, f32[1,2048]{1,0:T(1,128)}, f32[1,2048]{1,0:T(1,128)S(1)}, f32[1,2048]{1,0:T(1,128)}...) fusion(f32[3,2048]{1,0:T(4,128)S(1)} %slice_exponential_fusion,, ...), kind=kLoop, calls=%fused_computation.586 | loop fusion | flops 159744 | bytes 213040 | tf_op jit(solution)/shard_map/jvp()/div | solution.py:157
  61.3 5.5 %gather_fusion = f32[2048,9]{1,0:T(8,128)S(1)} fusion(f32[9,2048]{0,1:T(8,128)S(1)} %copy.299, s32[2048]{0:T(1024)S(1)} %broadcast_clamp_fusion), kind=kCustom, calls=%fused_computation | custom fusion | bytes 155648 | tf_op jit(solution)/shard_map/jvp()/gather | solution.py:264
  68.6 6.0 %all-to-all-start.1 = ((f32[8,9,256]{2,1,0:T(8,128)}), f32[8,9,256]{2,1,0:T(8,128)S(1)}, u32[]{:S(2)}, u32[]{:S(2)}) async-start(f32[8,9,256]{2,1,0:T(8,128)} %copy.301), calls=%async_computation.1 | async-start | bytes 262144 | tf_op jit(solution)/shard_map/all_to_all | solution.py:269
  75.1 6.9 %all-to-all-done.1 = f32[8,9,256]{2,1,0:T(8,128)S(1)} async-done(((f32[8,9,256]{2,1,0:T(8,128)}), f32[8,9,256]{2,1,0:T(8,128)S(1)}, u32[]{:S(2)}, u32[]{:S(2)}) %all-to-all-start.1) | async-done | bytes 73760 | tf_op jit(solution)/shard_map/all_to_all | solution.py:269
  84.6 3.7 %fusion.30 = f32[128,3,128]{2,1,0:T(4,128)S(1)} fusion(f32[3,128,16]{2,0,1:T(4,128)S(1)} %bitcast.204, f32[128,16]{1,0:T(8,128)S(1)} %bitcast.169, f32[128,16,128]{2,0,1:T(8,128)S(1)} %fusion.26, f32[128,16]{1,0:T(8,128)S(1)} %bitcast.174, f32[128,16]{1,0:T(8,128)S(1)} %bitcast.179, f32[128,128]{1,0:T(8,128)S(1)} %get-tuple-element.200, ...), kind=kOutput, calls=%fused_computation.64 | convolution fusion | flops 13631488 | bytes 1449984 | tf_op jit(solution)/shard_map/jvp(skp,csk->scp)/dot_general | solution.py:182
  93.5 2.1 collective-permute-start
  98.8 3.3 %collective-permute-done.1 = f32[6,5,512]{2,1,0:T(8,128)S(1)} collective-permute-done((f32[6,5,512]{2,1,0:T(8,128)S(1)}, f32[6,5,512]{2,1,0:T(8,128)S(1)}, u32[]{:S(2)}, u32[]{:S(2)}) %collective-permute-start.1) | collective-permute-done | bytes 61472 | tf_op jit(solution)/shard_map/ppermute | solution.py:40
  111.1 4.8 %collective-permute-start.3 = (f32[3,5,512]{2,1,0:T(8,128)S(1)}, f32[3,5,512]{2,1,0:T(8,128)S(1)}, u32[]{:S(2)}, u32[]{:S(2)}) collective-permute-start(f32[3,5,512]{2,1,0:T(8,128)S(1)} %get-tuple-element.131), channel_id=1, source_target_pairs={{0,4},{4,8},{8,12},{12,16},{16,20},{20,24},{24,28},{1,5},{5,9},{9,... | collective-permute-start | bytes 92168 | tf_op jit(solution)/shard_map/ppermute | solution.py:48
  124.2 4.2 %convolution_bitcast_fusion.1 = f32[3,128,16]{2,0,1:T(4,128)S(1)} fusion(f32[128,16]{1,0:T(8,128)S(1)} %bitcast.170, f32[128,16,128]{2,0,1:T(8,128)S(1)} %copy-done.3, f32[128,3,128]{2,0,1:T(8,128)S(1)} %split.13, f32[128,16]{1,0:T(8,128)S(1)} %bitcast.175, f32[128,16]{1,0:T(8,128)S(1)} %bitcast.180, f32[128,128]{1,0:T(8,128)S(1)} %copy-done.18, ...), kind=kOutput, calls=%fused_computation.18 | convolution fusion | flops 13631488 | bytes 1449984 | tf_op jit(solution)/shard_map/transpose(jvp(skp,csk->scp))/dot_general | solution.py:182
  128.4 4.0 %multiply_multiply_fusion = (f32[128,16,128]{2,1,0:T(8,128)S(1)}, f32[128,16,128]{2,1,0:T(8,128)S(1)}) fusion(f32[128,16]{1,0:T(8,128)S(1)} %bitcast.171, f32[128,16,128]{2,0,1:T(8,128)S(1)} %copy-done.3, f32[128,16]{1,0:T(8,128)S(1)} %bitcast.176, f32[128,16]{1,0:T(8,128)S(1)} %bitcast.181, f32[128,128]{1,0:T(8,128)S(1)} %copy-done.18, ...), kind=kOutput, calls=%fused_computation.50 | convolution fusion | flops 13893632 | bytes 3547136 | tf_op jit(solution)/shard_map/transpose(jvp(skp,csk->scp))/dot_general | solution.py:182
  132.7 5.5 %fusion.15 = (f32[128,16]{1,0:T(8,128)S(1)}, f32[128,16]{1,0:T(8,128)S(1)}, f32[128,16]{1,0:T(8,128)S(1)}, f32[128,16]{1,0:T(8,128)S(1)}, f32[128,16]{1,0:T(8,128)S(1)}, /*index=5*/f32[128,16]{1,0:T(8,128)S(1)}) fusion(f32[128,16]{1,0:T(8,128)S(1)} %bitcast.182, f32[128,128]{1,0:T(8,128)S(1)} %copy-done.18, f32[128,16]{1,0:T(8,128)S(1)} %bitcast.177, ...), kind=kLoop, calls=%fused_computation.32 | loop fusion | flops 13357056 | bytes 3440640 | tf_op jit(solution)/shard_map/transpose(jvp())/reduce_sum | solution.py:176
  140.3 6.8 %all-to-all-start.2 = ((f32[8,9,256]{2,1,0:T(8,128)}), f32[8,9,256]{2,1,0:T(8,128)S(1)}, u32[]{:S(2)}, u32[]{:S(2)}) async-start(f32[8,9,256]{2,1,0:T(8,128)} %copy.321), calls=%async_computation.2 | async-start | bytes 262144 | tf_op jit(solution)/shard_map/all_to_all | solution.py:301
  147.8 6.6 %all-to-all-done.2 = f32[8,9,256]{2,1,0:T(8,128)S(1)} async-done(((f32[8,9,256]{2,1,0:T(8,128)}), f32[8,9,256]{2,1,0:T(8,128)S(1)}, u32[]{:S(2)}, u32[]{:S(2)}) %all-to-all-start.2) | async-done | bytes 73760 | tf_op jit(solution)/shard_map/all_to_all | solution.py:301
  156.5 12.3 %scatter_custom_fusion = f32[9,2048]{0,1:T(8,128)S(1)} fusion(s32[2048]{0:T(1024)} %copy-done.36, f32[2048,9]{1,0:T(8,128)} %bitcast.166, f32[]{:T(128)} %constant.222.clone.1), kind=kCustom, calls=%fused_computation.61 | custom fusion | flops 18432 | bytes 74240 | tf_op jit(solution)/shard_map/transpose(jvp())/scatter-add | solution.py:264
  170.2 3.7 %fusion.270 = (f32[1,2048]{0,1:T(8,128)}, f32[1,2048]{0,1:T(8,128)}, f32[1,2048]{0,1:T(8,128)}, f32[1,2048]{0,1:T(8,128)}, f32[1,2048]{0,1:T(8,128)S(1)}, /*index=5*/f32[1,2048]{0,1:T(8,128)}) fusion(f32[9,2048]{0,1:T(8,128)S(1)} %scatter_custom_fusion), kind=kLoop, calls=%fused_computation.587 | loop fusion | bytes 98304 | tf_op jit(solution)/shard_map/transpose(jvp())/unstack | solution.py:156
  183.3 4.0 %add_add_fusion.6 = (f32[1,2048]{1,0:T(1,128)S(1)}, f32[1,2048]{1,0:T(1,128)S(1)}, f32[1,2048]{1,0:T(1,128)S(1)}, f32[1,2048]{1,0:T(1,128)S(1)}, f32[1,2048]{1,0...) fusion(f32[4,2048]{1,0:T(4,128)S(1)} %slice_divide_fusion, ...), kind=kLoop, calls=%fused_computation.445 | loop fusion | flops 167936 | bytes 237592 | tf_op jit(solution)/shard_map/transpose(jvp())/add_any | solution.py:113
  187.4 2.5 %multiply_add_fusion.8 = f32[1,2048]{1,0:T(1,128)S(1)} fusion(f32[1,2048]{1,0:T(1,128)S(1)} %get-tuple-element.62, f32[1,2048]{1,0:T(1,128)S(1)} %get-tuple-element.67, f32[1,2048]{1,0:T(1,128)S(1)} %get-tuple-element.66, f32[1,2048]{1,0:T(1,128)S(1)} %get-tuple-element.63, f32[1,2048]{1,0:T(1,128)S(1)} %get-tuple-element.65, ...), kind=kLoop, calls=%fused_computation.469 | loop fusion | flops 65536 | bytes 139280 | tf_op jit(solution)/shard_map/transpose(jvp())/add_any | solution.py:114
  189.9 2.7 %add_add_fusion.5 = f32[1,2048]{1,0:T(1,128)S(1)} fusion(f32[1,2048]{1,0:T(1,128)S(1)} %get-tuple-element.62, f32[1,2048]{1,0:T(1,128)S(1)} %get-tuple-element.67, f32[1,2048]{1,0:T(1,128)S(1)} %get-tuple-element.66, f32[1,2048]{1,0:T(1,128)S(1)} %get-tuple-element.64, f32[1,2048]{1,0:T(1,128)S(1)} %get-tuple-element.65, ...), kind=kLoop, calls=%fused_computation.444 | loop fusion | flops 65536 | bytes 139280 | tf_op jit(solution)/shard_map/transpose(jvp())/add_any | solution.py:113
  197.5 3.8 %multiply_add_fusion.12 = (f32[1,2048]{1,0:T(1,128)S(1)}, f32[1,2048]{1,0:T(1,128)S(1)}, f32[1,2048]{1,0:T(1,128)S(1)}, f32[1,2048]{1,0:T(1,128)S(1)}) fusion(f32[1,2048]{1,0:T(1,128)S(1)} %copy.356, f32[1,2048]{1,0:T(1,128)S(1)} %copy.355, f32[]{:T(128)} %bitcast.52, f32[]{:T(128)} %bitcast.49, f32[]{:T(128)} %bitcast.48, f32[]{:T(128)} %bitcast.51, ...), kind=kLoop, calls=%fused_computation.483 | loop fusion | flops 16384 | bytes 49176 | tf_op jit(solution)/shard_map/transpose(jvp())/add_any | solution.py:150
  204.2 18.8 %psum.15 = f32[]{:T(128)} all-reduce(f32[]{:T(128)} %get-tuple-element.56), channel_id=1, replica_groups=mesh['space'=8,'view'=4] {'space'}, use_global_device_ids=true, to_apply=%region_17.18 | all-reduce | flops 1 | bytes 8 | tf_op jit(solution)/shard_map/psum | solution.py:304
  223.7 10.8 %all-reduce.101.cloned.1.call-done = f32[59,2048]{1,0:T(8,128)} async-done(((f32[59,2048]{1,0:T(8,128)}), f32[59,2048]{1,0:T(8,128)}) %all-reduce.101.cloned.1.call-update) | async-done | bytes 483344 | tf_op jit(solution)/shard_map/psum | solution.py:303
  234.5 1.9 copy.406
  (279 shorter events, 67.3 us)
Async XLA Ops:
  9.9 58.7 %all-to-all-start = ((s32[8,1,16]{2,1,0:T(1,128)}), s32[8,1,16]{2,1,0:T(1,128)S(1)}, u32[]{:S(2)}, u32[]{:S(2)}) async-start(s32[8,1,16]{2,1,0:T(1,128)} %bitcast.45), calls=%async_computation | async-start | bytes 8192 | tf_op jit(solution)/shard_map/all_to_all | solution.py:270
  38.9 13.3 %copy-start.31 = (f32[2048]{0:T(1024)}, f32[2048]{0:T(1024)S(1)}, u32[]{:S(2)}) copy-start(f32[2048]{0:T(1024)S(1)} %multiply_reduce_fusion.6) | copy-start | bytes 24580
  43.7 17.0 %copy-start.33 = (f32[1,2048]{1,0:T(1,128)}, f32[1,2048]{1,0:T(1,128)S(1)}, u32[]{:S(2)}) copy-start(f32[1,2048]{1,0:T(1,128)S(1)} %get-tuple-element.121) | copy-start | bytes 24580
  68.6 19.8 %copy-start.27 = (s32[8,1,16]{2,1,0:T(1,128)}, s32[8,1,16]{2,1,0:T(1,128)S(1)}, u32[]{:S(2)}) copy-start(s32[8,1,16]{2,1,0:T(1,128)S(1)} %all-to-all-done) | copy-start | bytes 1540
  68.6 13.3 %all-to-all-start.1 = ((f32[8,9,256]{2,1,0:T(8,128)}), f32[8,9,256]{2,1,0:T(8,128)S(1)}, u32[]{:S(2)}, u32[]{:S(2)}) async-start(f32[8,9,256]{2,1,0:T(8,128)} %copy.301), calls=%async_computation.1 | async-start | bytes 262144 | tf_op jit(solution)/shard_map/all_to_all | solution.py:269
  75.0 9.5 %copy-start.17 = (f32[128,128]{1,0:T(8,128)}, f32[128,128]{1,0:T(8,128)S(1)}, u32[]{:S(2)}) copy-start(f32[128,128]{1,0:T(8,128)S(1)} %get-tuple-element.200) | copy-start | bytes 196612
  75.0 9.5 %copy-start.19 = (f32[128,128]{1,0:T(8,128)}, f32[128,128]{1,0:T(8,128)S(1)}, u32[]{:S(2)}) copy-start(f32[128,128]{1,0:T(8,128)S(1)} %get-tuple-element.201) | copy-start | bytes 196612
  82.3 2.3 copy-start.7
  84.5 3.8 %copy-start.2 = (f32[128,16,128]{2,0,1:T(8,128)}, f32[128,16,128]{2,0,1:T(8,128)S(1)}, u32[]{:S(2)}) copy-start(f32[128,16,128]{2,0,1:T(8,128)S(1)} %fusion.26) | copy-start | bytes 3145732
  93.5 5.3 %collective-permute-start = (f32[6,5,512]{2,1,0:T(8,128)S(1)}, f32[6,5,512]{2,1,0:T(8,128)S(1)}, u32[]{:S(2)}, u32[]{:S(2)}) collective-permute-start(f32[6,5,512]{2,1,0:T(8,128)S(1)} %get-tuple-element.148), channel_id=1, source_target_pairs={{0,4},{4,8},{8,12},{12,16},{16,20},{20,24},{24,28},{1,5},{5,9},{9,... | collective-permute-start | bytes 184328 | tf_op jit(solution)/shard_map/ppermute | solution.py:39
  95.6 6.5 %collective-permute-start.1 = (f32[6,5,512]{2,1,0:T(8,128)S(1)}, f32[6,5,512]{2,1,0:T(8,128)S(1)}, u32[]{:S(2)}, u32[]{:S(2)}) collective-permute-start(f32[6,5,512]{2,1,0:T(8,128)S(1)} %get-tuple-element.149), channel_id=1, source_target_pairs={{4,0},{8,4},{12,8},{16,12},{20,16},{24,20},{28,24},{5,1},{9,5},{13... | collective-permute-start | bytes 184328 | tf_op jit(solution)/shard_map/ppermute | solution.py:40
  109.8 6.1 %collective-permute-start.2 = (f32[3,5,512]{2,1,0:T(8,128)S(1)}, f32[3,5,512]{2,1,0:T(8,128)S(1)}, u32[]{:S(2)}, u32[]{:S(2)}) collective-permute-start(f32[3,5,512]{2,1,0:T(8,128)S(1)} %get-tuple-element.132), channel_id=1, source_target_pairs={{4,0},{8,4},{12,8},{16,12},{20,16},{24,20},{28,24},{5,1},{9,5},{13... | collective-permute-start | bytes 92168 | tf_op jit(solution)/shard_map/ppermute | solution.py:48
  111.1 6.3 %collective-permute-start.3 = (f32[3,5,512]{2,1,0:T(8,128)S(1)}, f32[3,5,512]{2,1,0:T(8,128)S(1)}, u32[]{:S(2)}, u32[]{:S(2)}) collective-permute-start(f32[3,5,512]{2,1,0:T(8,128)S(1)} %get-tuple-element.131), channel_id=1, source_target_pairs={{0,4},{4,8},{8,12},{12,16},{16,20},{20,24},{24,28},{1,5},{5,9},{9,... | collective-permute-start | bytes 92168 | tf_op jit(solution)/shard_map/ppermute | solution.py:48
  124.2 4.2 %copy-start.24 = (f32[3,8,16,16]{3,0,2,1:T(4,128)S(1)}, f32[3,8,16,16]{3,0,2,1:T(4,128)}, u32[]{:S(2)}) copy-start(f32[3,8,16,16]{3,0,2,1:T(4,128)} %copy-done.23) | copy-start | bytes 73732
  140.3 6.8 %copy-start.54 = (f32[16]{0:T(128)S(1)}, f32[16]{0:T(128)}, u32[]{:S(2)}) copy-start(f32[16]{0:T(128)} %copy-done.53) | copy-start | bytes 196
  140.3 14.1 %all-to-all-start.2 = ((f32[8,9,256]{2,1,0:T(8,128)}), f32[8,9,256]{2,1,0:T(8,128)S(1)}, u32[]{:S(2)}, u32[]{:S(2)}) async-start(f32[8,9,256]{2,1,0:T(8,128)} %copy.321), calls=%async_computation.2 | async-start | bytes 262144 | tf_op jit(solution)/shard_map/all_to_all | solution.py:301
  147.1 87.4 %all-reduce.101.cloned.1.call-start = ((), (), s32[]{:S(2)}) async-start(), calls=%async_computation.3 | async-start | bytes 1048576 | tf_op jit(solution)/shard_map/psum | solution.py:303
  175.6 2.6 %copy-start.1 = (f32[1,2048]{0,1:T(8,128)S(1)}, f32[1,2048]{0,1:T(8,128)}, u32[]{:S(2)}) copy-start(f32[1,2048]{0,1:T(8,128)} %get-tuple-element.106) | copy-start | bytes 24580
  178.4 3.4 %copy-start = (f32[1,2048]{0,1:T(8,128)S(1)}, f32[1,2048]{0,1:T(8,128)}, u32[]{:S(2)}) copy-start(f32[1,2048]{0,1:T(8,128)} %get-tuple-element.108) | copy-start | bytes 24580
  182.2 5.1 %copy-start.42 = (f32[1,2048]{1,0:T(1,128)S(1)}, f32[1,2048]{1,0:T(1,128)}, u32[]{:S(2)}) copy-start(f32[1,2048]{1,0:T(1,128)} %get-tuple-element.100) | copy-start | bytes 24580
  182.2 5.1 %copy-start.41 = (f32[1,2048]{1,0:T(1,128)S(1)}, f32[1,2048]{1,0:T(1,128)}, u32[]{:S(2)}) copy-start(f32[1,2048]{1,0:T(1,128)} %get-tuple-element.102) | copy-start | bytes 24580
  182.2 7.7 %copy-start.40 = (f32[1,2048]{1,0:T(1,128)S(1)}, f32[1,2048]{1,0:T(1,128)}, u32[]{:S(2)}) copy-start(f32[1,2048]{1,0:T(1,128)} %get-tuple-element.95) | copy-start | bytes 24580
  187.2 10.1 %copy-start.4 = (f32[48,2048]{1,0:T(8,128)S(1)}, f32[48,2048]{1,0:T(8,128)}, u32[]{:S(2)}) copy-start(f32[48,2048]{1,0:T(8,128)} %broadcast_in_dim.33) | copy-start | bytes 1179652
  189.9 2.7 %copy-start.39 = (f32[1,2048]{1,0:T(1,128)S(1)}, f32[1,2048]{1,0:T(1,128)}, u32[]{:S(2)}) copy-start(f32[1,2048]{1,0:T(1,128)} %get-tuple-element.98) | copy-start | bytes 24580
  (47 other events, 47.6 us)
Sparse Core Ops, SparseCore 0:
  203.3 31.1 all-reduce.100
where the time goes:
time: 246 us; the launch traced here: 244 us
  other arithmetic  61 us (25%)
  local copies, waits for them, and re-layouts  49.4 us (20%)
  between operations  40.5 us (16%)
  waiting for transfers between devices  30.6 us (12%)
  starting transfers between devices  29.8 us (12%)
  blocking collectives  18.8 us (8%)
  matrix products  14.2 us (6%)
    unnamed x135, local copies, waits for them, and re-layouts  21.7 us
    psum x1, blocking collectives, shards(): loss_sum = lax.psum(own_loss, 'space')  18.8 us
    scatter-add x1, other arithmetic, sender_side(): picked = record_in[:, lists]  12.3 us
    dot_general x3, matrix products, render(): jnp.einsum('skp,csk->scp', weights, gathered[6:9], precision=HIGHEST)  11.8 us
    psum x1, waiting for transfers between devices, shards(): grad_params = lax.psum(pull_project(grad_records)[0], 'view')  10.8 us
    all_to_all x1, starting transfers between devices, shards(): lax.all_to_all(target_ids, 'space', split_axis=0, concat_axis=0, tiled=True)  7.31 us
    all_to_all x1, waiting for transfers between devices, shards(): lax.all_to_all(message, 'space', split_axis=0, concat_axis=0, tiled=True)  6.88 us
    all_to_all x1, starting transfers between devices, shards(): lax.all_to_all(grad_received, 'space', split_axis=0, concat_axis=0, tiled...  6.8 us
  transfers between devices with their start and end apart: 8, of which 6 were waited for; matrix products, arithmetic and copies ran while one was open for 11% of the time, Pallas kernels for 0%

commit v1 on v0

--- a/solution.py
+++ b/solution.py
@@ -300,7 +300,7 @@
     grad_received = pull_owner(grad_strip)[0]
     returned = lax.all_to_all(grad_received, "space", split_axis=0, concat_axis=0, tiled=True)
     grad_records = pull_sender(returned)[0]
-    grad_params = lax.psum(pull_project(grad_records)[0], "view")
+    grad_params = jnp.sum(lax.all_gather(pull_project(grad_records)[0], "view"), axis=0)
     loss_sum = lax.psum(own_loss, "space")
     loss_value = (loss_sum / (3.0 * height_px * width_px)).reshape(1)
     return (grad_params, strip[None], loss_value)

time: 246 us -> 234 us (0.951)
  local copies, waits for them, and re-layouts: 49.4 us -> 37 us
  waiting for transfers between devices: 30.6 us -> 19.8 us
  other arithmetic: 61 us -> 70.8 us
    unnamed x135 -> x88, local copies, waits for them, and re-layouts: 21.7 us -> 9.24 us
    psum x1 -> x0, waiting for transfers between devices: 10.8 us -> none  [shards(): grad_params = lax.psum(pull_project(grad_records)[0], 'view')]
    mul x6, other arithmetic: 0.07 us -> 2.86 us  [project(): (turn[row, 0] * spin[0][col] + turn[row, 1] * spin[1][col] + turn[row, 2]...]
    reduce_sum x0 -> x1, other arithmetic: none -> 2.56 us  [shards(): jnp.sum(lax.all_gather(pull_project(grad_records)[0], 'view'), axis=0)]
  transfers between devices with their start and end apart: 8 -> 8, of which waited for: 6 -> 5; matrix products, arithmetic and copies ran while one was open for 11% -> 13% of each run, Pallas kernels for 0% -> 0%
where the time goes in v1:
time: 234 us; the launch traced here: 232 us
  other arithmetic  70.8 us (30%)
  between operations  40.6 us (17%)
  local copies, waits for them, and re-layouts  37 us (16%)
  starting transfers between devices  29.7 us (13%)
  waiting for transfers between devices  19.8 us (8%)
  blocking collectives  18.8 us (8%)
  matrix products  15.6 us (7%)
    psum x1, blocking collectives, shards(): loss_sum = lax.psum(own_loss, 'space')  18.8 us
    scatter-add x1, other arithmetic, sender_side(): picked = record_in[:, lists]  12.3 us
    dot_general x3, matrix products, render(): jnp.einsum('skp,csk->scp', weights, gathered[6:9], precision=HIGHEST)  11.8 us
    unnamed x88, local copies, waits for them, and re-layouts  9.24 us
    all_to_all x1, starting transfers between devices, shards(): lax.all_to_all(target_ids, 'space', split_axis=0, concat_axis=0, tiled=True)  7.31 us
    all_to_all x1, waiting for transfers between devices, shards(): lax.all_to_all(message, 'space', split_axis=0, concat_axis=0, tiled=True)  6.88 us
    all_to_all x1, starting transfers between devices, shards(): lax.all_to_all(grad_received, 'space', split_axis=0, concat_axis=0, tiled...  6.67 us
    all_to_all x1, waiting for transfers between devices, shards(): lax.all_to_all(grad_received, 'space', split_axis=0, concat_axis=0, tiled...  6.59 us
  transfers between devices with their start and end apart: 8, of which 5 were waited for; matrix products, arithmetic and copies ran while one was open for 13% of the time, Pallas kernels for 0%

profile of v1, /device:TPU:0, one launch (start us, length us, event | category | flops | bytes accessed | tf_op | source)
XLA Modules:
  0.0 232.3 jit_solution(13551380403058516265)
XLA Ops:
  10.4 7.3 %all-to-all-start = ((s32[8,1,16]{2,1,0:T(1,128)}), s32[8,1,16]{2,1,0:T(1,128)S(1)}, u32[]{:S(2)}, u32[]{:S(2)}) async-start(s32[8,1,16]{2,1,0:T(1,128)} %bitcast.45), calls=%async_computation | async-start | bytes 8192 | tf_op jit(solution)/shard_map/all_to_all | solution.py:270
  39.7 4.8 %add_divide_fusion = (f32[1,2048]{1,0:T(1,128)S(1)}, f32[1,2048]{1,0:T(1,128)S(1)}, f32[1,2048]{1,0:T(1,128)S(1)}) fusion(f32[59,2048]{1,0:T(8,128)} %param.12, f32[]{:T(128)} %bitcast.50, f32[]{:T(128)} %bitcast.49, f32[]{:T(128)} %bitcast.48, f32[]{:T(128)} %bitcast.53, f32[]{:T(128)} %bitcast.52, f32[]{:T(128)} %bitcast.51), kind=kLoop, calls=%fused_computation.484 | loop fusion | flops 34816 | bytes 57368 | tf_op jit(solution)/shard_map/jvp()/div | solution.py:152
  56.4 4.6 %fusion.269 = (f32[1,2048]{1,0:T(1,128)S(1)}, f32[1,2048]{1,0:T(1,128)S(1)}, f32[1,2048]{1,0:T(1,128)}, f32[1,2048]{1,0:T(1,128)S(1)}, f32[1,2048]{1,0:T(1,128)}...) fusion(f32[3,2048]{1,0:T(4,128)S(1)} %slice_exponential_fusion,, ...), kind=kLoop, calls=%fused_computation.586 | loop fusion | flops 159744 | bytes 213040 | tf_op jit(solution)/shard_map/jvp()/div | solution.py:157
  61.6 5.5 %gather_fusion = f32[2048,9]{1,0:T(8,128)S(1)} fusion(f32[9,2048]{0,1:T(8,128)S(1)} %copy.301, s32[2048]{0:T(1024)S(1)} %broadcast_clamp_fusion), kind=kCustom, calls=%fused_computation | custom fusion | bytes 155648 | tf_op jit(solution)/shard_map/jvp()/gather | solution.py:264
  68.9 6.0 %all-to-all-start.1 = ((f32[8,9,256]{2,1,0:T(8,128)}), f32[8,9,256]{2,1,0:T(8,128)S(1)}, u32[]{:S(2)}, u32[]{:S(2)}) async-start(f32[8,9,256]{2,1,0:T(8,128)} %copy.303), calls=%async_computation.1 | async-start | bytes 262144 | tf_op jit(solution)/shard_map/all_to_all | solution.py:269
  75.4 6.9 %all-to-all-done.1 = f32[8,9,256]{2,1,0:T(8,128)S(1)} async-done(((f32[8,9,256]{2,1,0:T(8,128)}), f32[8,9,256]{2,1,0:T(8,128)S(1)}, u32[]{:S(2)}, u32[]{:S(2)}) %all-to-all-start.1) | async-done | bytes 73760 | tf_op jit(solution)/shard_map/all_to_all | solution.py:269
  84.9 3.7 %fusion.30 = f32[128,3,128]{2,1,0:T(4,128)S(1)} fusion(f32[3,128,16]{2,0,1:T(4,128)S(1)} %bitcast.206, f32[128,16]{1,0:T(8,128)S(1)} %bitcast.171, f32[128,16,128]{2,0,1:T(8,128)S(1)} %fusion.26, f32[128,16]{1,0:T(8,128)S(1)} %bitcast.176, f32[128,16]{1,0:T(8,128)S(1)} %bitcast.181, f32[128,128]{1,0:T(8,128)S(1)} %get-tuple-element.191, ...), kind=kOutput, calls=%fused_computation.64 | convolution fusion | flops 13631488 | bytes 1449984 | tf_op jit(solution)/shard_map/jvp(skp,csk->scp)/dot_general | solution.py:182
  91.4 2.1 collective-permute-start
  96.8 3.3 %collective-permute-done.1 = f32[6,5,512]{2,1,0:T(8,128)S(1)} collective-permute-done((f32[6,5,512]{2,1,0:T(8,128)S(1)}, f32[6,5,512]{2,1,0:T(8,128)S(1)}, u32[]{:S(2)}, u32[]{:S(2)}) %collective-permute-start.1) | collective-permute-done | bytes 61472 | tf_op jit(solution)/shard_map/ppermute | solution.py:40
  109.1 4.8 %collective-permute-start.3 = (f32[3,5,512]{2,1,0:T(8,128)S(1)}, f32[3,5,512]{2,1,0:T(8,128)S(1)}, u32[]{:S(2)}, u32[]{:S(2)}) collective-permute-start(f32[3,5,512]{2,1,0:T(8,128)S(1)} %get-tuple-element.122), channel_id=1, source_target_pairs={{0,4},{4,8},{8,12},{12,16},{16,20},{20,24},{24,28},{1,5},{5,9},{9,... | collective-permute-start | bytes 92168 | tf_op jit(solution)/shard_map/ppermute | solution.py:48
  120.8 4.2 %convolution_bitcast_fusion.1 = f32[3,128,16]{2,0,1:T(4,128)S(1)} fusion(f32[128,16]{1,0:T(8,128)S(1)} %bitcast.172, f32[128,16,128]{2,0,1:T(8,128)S(1)} %copy-done.2, f32[128,3,128]{2,0,1:T(8,128)S(1)} %split.13, f32[128,16]{1,0:T(8,128)S(1)} %bitcast.177, f32[128,16]{1,0:T(8,128)S(1)} %bitcast.182, f32[128,128]{1,0:T(8,128)S(1)} %copy-done.12, ...), kind=kOutput, calls=%fused_computation.18 | convolution fusion | flops 13631488 | bytes 1449984 | tf_op jit(solution)/shard_map/transpose(jvp(skp,csk->scp))/dot_general | solution.py:182
  125.0 4.0 %multiply_multiply_fusion = (f32[128,16,128]{2,1,0:T(8,128)S(1)}, f32[128,16,128]{2,1,0:T(8,128)S(1)}) fusion(f32[128,16]{1,0:T(8,128)S(1)} %bitcast.173, f32[128,16,128]{2,0,1:T(8,128)S(1)} %copy-done.2, f32[128,16]{1,0:T(8,128)S(1)} %bitcast.178, f32[128,16]{1,0:T(8,128)S(1)} %bitcast.183, f32[128,128]{1,0:T(8,128)S(1)} %copy-done.12, ...), kind=kOutput, calls=%fused_computation.50 | convolution fusion | flops 13893632 | bytes 3547136 | tf_op jit(solution)/shard_map/transpose(jvp(skp,csk->scp))/dot_general | solution.py:182
  129.3 5.5 %fusion.15 = (f32[128,16]{1,0:T(8,128)S(1)}, f32[128,16]{1,0:T(8,128)S(1)}, f32[128,16]{1,0:T(8,128)S(1)}, f32[128,16]{1,0:T(8,128)S(1)}, f32[128,16]{1,0:T(8,128)S(1)}, /*index=5*/f32[128,16]{1,0:T(8,128)S(1)}) fusion(f32[128,16]{1,0:T(8,128)S(1)} %bitcast.184, f32[128,128]{1,0:T(8,128)S(1)} %copy-done.12, f32[128,16]{1,0:T(8,128)S(1)} %bitcast.179, ...), kind=kLoop, calls=%fused_computation.32 | loop fusion | flops 13357056 | bytes 3440640 | tf_op jit(solution)/shard_map/transpose(jvp())/reduce_sum | solution.py:176
  136.9 6.7 %all-to-all-start.2 = ((f32[8,9,256]{2,1,0:T(8,128)}), f32[8,9,256]{2,1,0:T(8,128)S(1)}, u32[]{:S(2)}, u32[]{:S(2)}) async-start(f32[8,9,256]{2,1,0:T(8,128)} %copy.323), calls=%async_computation.2 | async-start | bytes 262144 | tf_op jit(solution)/shard_map/all_to_all | solution.py:301
  144.3 6.6 %all-to-all-done.2 = f32[8,9,256]{2,1,0:T(8,128)S(1)} async-done(((f32[8,9,256]{2,1,0:T(8,128)}), f32[8,9,256]{2,1,0:T(8,128)S(1)}, u32[]{:S(2)}, u32[]{:S(2)}) %all-to-all-start.2) | async-done | bytes 73760 | tf_op jit(solution)/shard_map/all_to_all | solution.py:301
  151.2 1.8 copy.356
  153.0 12.3 %scatter_custom_fusion = f32[9,2048]{0,1:T(8,128)S(1)} fusion(s32[2048]{0:T(1024)} %copy-done.30, f32[2048,9]{1,0:T(8,128)} %bitcast.168, f32[]{:T(128)} %constant.222.clone.1), kind=kCustom, calls=%fused_computation.61 | custom fusion | flops 18432 | bytes 74240 | tf_op jit(solution)/shard_map/transpose(jvp())/scatter-add | solution.py:264
  166.7 3.7 %fusion.270 = (f32[1,2048]{0,1:T(8,128)}, f32[1,2048]{0,1:T(8,128)}, f32[1,2048]{0,1:T(8,128)}, f32[1,2048]{0,1:T(8,128)}, f32[1,2048]{0,1:T(8,128)S(1)}, /*index=5*/f32[1,2048]{0,1:T(8,128)}) fusion(f32[9,2048]{0,1:T(8,128)S(1)} %scatter_custom_fusion), kind=kLoop, calls=%fused_computation.587 | loop fusion | bytes 98304 | tf_op jit(solution)/shard_map/transpose(jvp())/unstack | solution.py:156
  180.2 4.7 %add_add_fusion.6 = (f32[1,2048]{1,0:T(1,128)S(1)}, f32[1,2048]{1,0:T(1,128)S(1)}, f32[1,2048]{1,0:T(1,128)S(1)}, f32[1,2048]{1,0:T(1,128)S(1)}, f32[1,2048]{1,0...) fusion(f32[4,2048]{1,0:T(4,128)S(1)} %slice_divide_fusion, ...), kind=kLoop, calls=%fused_computation.445 | loop fusion | flops 167936 | bytes 237592 | tf_op jit(solution)/shard_map/transpose(jvp())/add_any | solution.py:113
  185.0 2.5 %multiply_add_fusion.8 = f32[1,2048]{1,0:T(1,128)S(1)} fusion(f32[1,2048]{1,0:T(1,128)S(1)} %get-tuple-element.53, f32[1,2048]{1,0:T(1,128)S(1)} %get-tuple-element.58, f32[1,2048]{1,0:T(1,128)S(1)} %get-tuple-element.57, f32[1,2048]{1,0:T(1,128)S(1)} %get-tuple-element.54, f32[1,2048]{1,0:T(1,128)S(1)} %get-tuple-element.56, ...), kind=kLoop, calls=%fused_computation.469 | loop fusion | flops 65536 | bytes 139280 | tf_op jit(solution)/shard_map/transpose(jvp())/add_any | solution.py:114
  188.2 2.6 %add_add_fusion.5 = f32[1,2048]{1,0:T(1,128)S(1)} fusion(f32[1,2048]{1,0:T(1,128)S(1)} %get-tuple-element.53, f32[1,2048]{1,0:T(1,128)S(1)} %get-tuple-element.58, f32[1,2048]{1,0:T(1,128)S(1)} %get-tuple-element.57, f32[1,2048]{1,0:T(1,128)S(1)} %get-tuple-element.55, f32[1,2048]{1,0:T(1,128)S(1)} %get-tuple-element.56, ...), kind=kLoop, calls=%fused_computation.444 | loop fusion | flops 65536 | bytes 139280 | tf_op jit(solution)/shard_map/transpose(jvp())/add_any | solution.py:113
  195.6 3.7 %multiply_add_fusion.12 = (f32[1,2048]{1,0:T(1,128)S(1)}, f32[1,2048]{1,0:T(1,128)S(1)}, f32[1,2048]{1,0:T(1,128)S(1)}, f32[1,2048]{1,0:T(1,128)S(1)}) fusion(f32[1,2048]{1,0:T(1,128)S(1)} %copy.361, f32[1,2048]{1,0:T(1,128)S(1)} %copy.360, f32[]{:T(128)} %bitcast.52, f32[]{:T(128)} %bitcast.49, f32[]{:T(128)} %bitcast.48, f32[]{:T(128)} %bitcast.51, ...), kind=kLoop, calls=%fused_computation.483 | loop fusion | flops 16384 | bytes 49176 | tf_op jit(solution)/shard_map/transpose(jvp())/add_any | solution.py:150
  202.3 18.8 %psum.7 = f32[]{:T(128)} all-reduce(f32[]{:T(128)} %get-tuple-element.47), channel_id=1, replica_groups=mesh['space'=8,'view'=4] {'space'}, use_global_device_ids=true, to_apply=%region_17.18 | all-reduce | flops 1 | bytes 8 | tf_op jit(solution)/shard_map/psum | solution.py:304
  221.8 2.6 %reduce_sum.154 = f32[59,2048]{1,0:T(8,128)} reduce(f32[4,59,2048]{2,1,0:T(8,128)} %all-gather.4.cloned.1.call-done, f32[]{:T(128)} %constant.222.clone.1), dimensions={0}, to_apply=%region_15.16 | reduce | flops 362496 | bytes 2416644 | tf_op jit(solution)/shard_map/reduce_sum | solution.py:303
  (233 shorter events, 63.1 us)
Async XLA Ops:
  10.4 58.5 %all-to-all-start = ((s32[8,1,16]{2,1,0:T(1,128)}), s32[8,1,16]{2,1,0:T(1,128)S(1)}, u32[]{:S(2)}, u32[]{:S(2)}) async-start(s32[8,1,16]{2,1,0:T(1,128)} %bitcast.45), calls=%async_computation | async-start | bytes 8192 | tf_op jit(solution)/shard_map/all_to_all | solution.py:270
  39.7 15.4 %copy-start.25 = (f32[2048]{0:T(1024)}, f32[2048]{0:T(1024)S(1)}, u32[]{:S(2)}) copy-start(f32[2048]{0:T(1024)S(1)} %multiply_reduce_fusion.6) | copy-start | bytes 24580
  44.5 16.5 %copy-start.27 = (f32[1,2048]{1,0:T(1,128)}, f32[1,2048]{1,0:T(1,128)S(1)}, u32[]{:S(2)}) copy-start(f32[1,2048]{1,0:T(1,128)S(1)} %get-tuple-element.112) | copy-start | bytes 24580
  55.4 11.7 %copy-start.30 = (s32[2048]{0:T(1024)}, s32[2048]{0:T(1024)S(1)}, u32[]{:S(2)}) copy-start(s32[2048]{0:T(1024)S(1)} %reshape.534) | copy-start | bytes 24580
  61.0 6.1 %copy-start.19 = (f32[1,2048]{1,0:T(1,128)}, f32[1,2048]{1,0:T(1,128)S(1)}, u32[]{:S(2)}) copy-start(f32[1,2048]{1,0:T(1,128)S(1)} %get-tuple-element.87) | copy-start | bytes 24580
  68.9 19.7 %copy-start.21 = (s32[8,1,16]{2,1,0:T(1,128)}, s32[8,1,16]{2,1,0:T(1,128)S(1)}, u32[]{:S(2)}) copy-start(s32[8,1,16]{2,1,0:T(1,128)S(1)} %all-to-all-done) | copy-start | bytes 1540
  68.9 13.3 %all-to-all-start.1 = ((f32[8,9,256]{2,1,0:T(8,128)}), f32[8,9,256]{2,1,0:T(8,128)S(1)}, u32[]{:S(2)}, u32[]{:S(2)}) async-start(f32[8,9,256]{2,1,0:T(8,128)} %copy.303), calls=%async_computation.1 | async-start | bytes 262144 | tf_op jit(solution)/shard_map/all_to_all | solution.py:269
  75.4 9.5 %copy-start.11 = (f32[128,128]{1,0:T(8,128)}, f32[128,128]{1,0:T(8,128)S(1)}, u32[]{:S(2)}) copy-start(f32[128,128]{1,0:T(8,128)S(1)} %get-tuple-element.191) | copy-start | bytes 196612
  75.4 9.5 %copy-start.13 = (f32[128,128]{1,0:T(8,128)}, f32[128,128]{1,0:T(8,128)S(1)}, u32[]{:S(2)}) copy-start(f32[128,128]{1,0:T(8,128)S(1)} %get-tuple-element.192) | copy-start | bytes 196612
  91.4 5.3 %collective-permute-start = (f32[6,5,512]{2,1,0:T(8,128)S(1)}, f32[6,5,512]{2,1,0:T(8,128)S(1)}, u32[]{:S(2)}, u32[]{:S(2)}) collective-permute-start(f32[6,5,512]{2,1,0:T(8,128)S(1)} %get-tuple-element.139), channel_id=1, source_target_pairs={{0,4},{4,8},{8,12},{12,16},{16,20},{20,24},{24,28},{1,5},{5,9},{9,... | collective-permute-start | bytes 184328 | tf_op jit(solution)/shard_map/ppermute | solution.py:39
  93.6 6.5 %collective-permute-start.1 = (f32[6,5,512]{2,1,0:T(8,128)S(1)}, f32[6,5,512]{2,1,0:T(8,128)S(1)}, u32[]{:S(2)}, u32[]{:S(2)}) collective-permute-start(f32[6,5,512]{2,1,0:T(8,128)S(1)} %get-tuple-element.140), channel_id=1, source_target_pairs={{4,0},{8,4},{12,8},{16,12},{20,16},{24,20},{28,24},{5,1},{9,5},{13... | collective-permute-start | bytes 184328 | tf_op jit(solution)/shard_map/ppermute | solution.py:40
  107.7 6.1 %collective-permute-start.2 = (f32[3,5,512]{2,1,0:T(8,128)S(1)}, f32[3,5,512]{2,1,0:T(8,128)S(1)}, u32[]{:S(2)}, u32[]{:S(2)}) collective-permute-start(f32[3,5,512]{2,1,0:T(8,128)S(1)} %get-tuple-element.123), channel_id=1, source_target_pairs={{4,0},{8,4},{12,8},{16,12},{20,16},{24,20},{28,24},{5,1},{9,5},{13... | collective-permute-start | bytes 92168 | tf_op jit(solution)/shard_map/ppermute | solution.py:48
  109.1 6.3 %collective-permute-start.3 = (f32[3,5,512]{2,1,0:T(8,128)S(1)}, f32[3,5,512]{2,1,0:T(8,128)S(1)}, u32[]{:S(2)}, u32[]{:S(2)}) collective-permute-start(f32[3,5,512]{2,1,0:T(8,128)S(1)} %get-tuple-element.122), channel_id=1, source_target_pairs={{0,4},{4,8},{8,12},{12,16},{16,20},{20,24},{24,28},{1,5},{5,9},{9,... | collective-permute-start | bytes 92168 | tf_op jit(solution)/shard_map/ppermute | solution.py:48
  134.9 8.7 %copy-start.38 = (f32[16]{0:T(128)S(1)}, f32[16]{0:T(128)}, u32[]{:S(2)}) copy-start(f32[16]{0:T(128)} %copy-done.37) | copy-start | bytes 196
  136.9 14.0 %all-to-all-start.2 = ((f32[8,9,256]{2,1,0:T(8,128)}), f32[8,9,256]{2,1,0:T(8,128)S(1)}, u32[]{:S(2)}, u32[]{:S(2)}) async-start(f32[8,9,256]{2,1,0:T(8,128)} %copy.323), calls=%async_computation.2 | async-start | bytes 262144 | tf_op jit(solution)/shard_map/all_to_all | solution.py:301
  143.6 78.2 %all-gather.4.cloned.1.call-start = ((), (), s32[]{:S(2)}) async-start(), calls=%async_computation.3 | async-start | bytes 2621440 | tf_op jit(solution)/shard_map/all_gather | solution.py:303
  172.3 6.5 %copy-start.20 = (f32[1,2048]{1,0:T(1,128)S(1)}, f32[1,2048]{1,0:T(1,128)}, u32[]{:S(2)}) copy-start(f32[1,2048]{1,0:T(1,128)} %copy-done.19) | copy-start | bytes 24580
  172.3 6.5 %copy-start.33 = (f32[1,2048]{1,0:T(1,128)S(1)}, f32[1,2048]{1,0:T(1,128)}, u32[]{:S(2)}) copy-start(f32[1,2048]{1,0:T(1,128)} %get-tuple-element.81) | copy-start | bytes 24580
  172.3 7.2 %copy-start = (f32[1,2048]{0,1:T(8,128)S(1)}, f32[1,2048]{0,1:T(8,128)}, u32[]{:S(2)}) copy-start(f32[1,2048]{0,1:T(8,128)} %get-tuple-element.99) | copy-start | bytes 24580
  175.5 9.3 %copy-start.32 = (f32[1,2048]{1,0:T(1,128)S(1)}, f32[1,2048]{1,0:T(1,128)}, u32[]{:S(2)}) copy-start(f32[1,2048]{1,0:T(1,128)} %get-tuple-element.91) | copy-start | bytes 24580
  175.5 9.4 %copy-start.31 = (f32[1,2048]{1,0:T(1,128)S(1)}, f32[1,2048]{1,0:T(1,128)}, u32[]{:S(2)}) copy-start(f32[1,2048]{1,0:T(1,128)} %get-tuple-element.93) | copy-start | bytes 24580
  177.1 15.8 %copy-start.29 = (f32[2048]{0:T(1024)S(1)}, f32[2048]{0:T(1024)}, u32[]{:S(2)}) copy-start(f32[2048]{0:T(1024)} %get-tuple-element.165) | copy-start | bytes 24580
  177.1 16.8 %copy-start.26 = (f32[2048]{0:T(1024)S(1)}, f32[2048]{0:T(1024)}, u32[]{:S(2)}) copy-start(f32[2048]{0:T(1024)} %copy-done.25) | copy-start | bytes 24580
  177.1 16.8 %copy-start.24 = (f32[2048]{0:T(1024)S(1)}, f32[2048]{0:T(1024)}, u32[]{:S(2)}) copy-start(f32[2048]{0:T(1024)} %copy-done.23) | copy-start | bytes 24580
  (24 other events, 42.8 us)
Sparse Core Ops, SparseCore 0:
  201.3 20.3 all-gather.3
